TPU v7x, 32 devices: a whole 2x2x4 slice. The times are simulated.
32 devices in a mesh: depth: 4 (over z), row: 4 (over x, core), col: 2 (over y).
Axes of the slice: x: 2, y: 2, z: 4, core: 2. Of those that a mesh axis runs over, the one named last changes fastest.
Arguments:
- acts: bfloat16 [2048, 4096], P(('depth', 'col'), 'row'), may hold values from -0.3125 to 0.3125
- grad_out: bfloat16 [2048, 14336], P(('depth', 'row'), 'col'), may hold values from -6 to 6
- weight: bfloat16 [4096, 14336], P('row', 'col'), may hold values from -0.046875 to 0.046875
Outputs:
- grad_acts: bfloat16 [2048, 4096], P(('depth', 'col'), 'row')
- grad_weight: bfloat16 [4096, 14336], P('row', 'col')
All inputs are finite; a program needn't handle non-finite values.
Results may differ from a plain program's by a relative error of at most 0.013.
Values may be sent and summed in bfloat16 or wider, within the bound.
A program may use at most 128 MiB of HBM per device.

v0:
```python
import jax
import jax.numpy as jnp
from jax import lax
from jax.sharding import PartitionSpec as P


def shards(acts, grad_out, weight):
    grad_rows = lax.all_gather(grad_out, "row", axis=0, tiled=True)
    grad_acts = lax.psum_scatter(
        lax.dot_general(
            grad_rows, weight, (((1,), (1,)), ((), ())), preferred_element_type=jnp.float32
        ).astype(jnp.bfloat16),
        "col",
        scatter_dimension=0,
        tiled=True,
    )
    partial_sum = lax.dot_general(
        lax.all_gather(acts, "col", axis=0, tiled=True),
        grad_rows,
        (((0,), (0,)), ((), ())),
        preferred_element_type=jnp.float32,
    )
    grad_weight = lax.psum(partial_sum.astype(jnp.bfloat16), "depth")
    return (grad_acts, grad_weight)


def solution(mesh):
    in_specs = (P(("depth", "col"), "row"), P(("depth", "row"), "col"), P("row", "col"))
    out_specs = (P(("depth", "col"), "row"), P("row", "col"))
    return jax.shard_map(shards, mesh=mesh, in_specs=in_specs, out_specs=out_specs, check_vma=False)
```

profile of v0, /device:TPU:0, one launch (start us, length us, event | category | flops | bytes accessed | tf_op | source)
XLA Modules:
  0.0 627.1 jit_solution(1887198143985389784)
XLA Ops:
  7.2 0.0 all-gather.3.cloned.1.call-start
  7.2 0.7 all-gather.3.cloned.1.call-update
  7.9 0.0 all-gather.5.cloned.1.call-start
  7.9 0.7 all-gather.5.cloned.1.call-update
  8.6 0.0 reduce-scatter.2.cloned.1.call-start
  8.7 55.9 %all-gather.3.cloned.1.call-done = bf16[512,7168]{1,0:T(8,128)(2,1)} async-done(((bf16[128,7168]{1,0:T(8,128)(2,1)}), bf16[512,7168]{1,0:T(8,128)(2,1)}) %all-gather.3.cloned.1.call-update) | async-done | bytes 7340048 | tf_op jit(solution)/shard_map/all_gather | solution.py:8
  64.6 14.0 %convolution_convert_fusion.1 = bf16[512,1024]{1,0:T(8,128)(2,1)} fusion(bf16[512,7168]{1,0:T(8,128)(2,1)} %all-gather.3.cloned.1.call-done, bf16[1024,7168]{1,0:T(8,128)(2,1)} %param.5), kind=kOutput, calls=%fused_computation.1 | convolution fusion | flops 7516717056 | bytes 23068672 | tf_op jit(solution)/shard_map/dot_general | solution.py:10
  78.6 0.0 reduce-scatter.2.cloned.1.call-update
  78.6 0.0 all-reduce.2.cloned.1.call-start
  78.7 8.8 %all-gather.5.cloned.1.call-done = bf16[512,1024]{1,0:T(8,128)(2,1)} async-done(((bf16[256,1024]{1,0:T(8,128)(2,1)}), bf16[512,1024]{1,0:T(8,128)(2,1)}) %all-gather.5.cloned.1.call-update) | async-done | bytes 1048592 | tf_op jit(solution)/shard_map/all_gather | solution.py:18
  87.5 13.4 %convolution_convert_fusion = bf16[1024,7168]{1,0:T(8,128)(2,1)} fusion(bf16[512,1024]{1,0:T(8,128)(2,1)} %all-gather.5.cloned.1.call-done, bf16[512,7168]{1,0:T(8,128)(2,1)} %all-gather.3.cloned.1.call-done), kind=kOutput, calls=%fused_computation | convolution fusion | flops 7523532800 | bytes 23068672 | tf_op jit(solution)/shard_map/dot_general | solution.py:17
  100.9 0.0 all-reduce.2.cloned.1.call-update
  100.9 9.8 %reduce-scatter.2.cloned.1.call-done = bf16[256,1024]{1,0:T(8,128)(2,1)} async-done(((bf16[512,1024]{1,0:T(8,128)(2,1)}), bf16[256,1024]{1,0:T(8,128)(2,1)}) %reduce-scatter.2.cloned.1.call-update) | async-done | bytes 524304 | tf_op jit(solution)/shard_map/reduce_scatter | solution.py:9
  110.7 496.7 %all-reduce.2.cloned.1.call-done = bf16[1024,7168]{1,0:T(8,128)(2,1)} async-done(((bf16[1024,7168]{1,0:T(8,128)(2,1)}), bf16[1024,7168]{1,0:T(8,128)(2,1)}) %all-reduce.2.cloned.1.call-update) | async-done | bytes 14680080 | tf_op jit(solution)/shard_map/psum | solution.py:23
  607.4 13.2 %copy.6 = bf16[1024,7168]{1,0:T(8,128)(2,1)} copy(bf16[1024,7168]{1,0:T(8,128)(2,1)} %all-reduce.2.cloned.1.call-done) | data formatting | bytes 29360128
Async XLA Ops:
  7.2 57.4 %all-gather.3.cloned.1.call-start = ((), (), s32[]{:S(2)}) async-start(), calls=%async_computation.1 | async-start | bytes 9175040 | tf_op jit(solution)/shard_map/all_gather | solution.py:8
  7.9 79.6 %all-gather.5.cloned.1.call-start = ((), (), s32[]{:S(2)}) async-start(), calls=%async_computation.3 | async-start | bytes 1572864 | tf_op jit(solution)/shard_map/all_gather | solution.py:18
  8.6 102.0 %reduce-scatter.2.cloned.1.call-start = ((), (), s32[]{:S(2)}) async-start(), calls=%async_computation.2 | async-start | bytes 1572864 | tf_op jit(solution)/shard_map/reduce_scatter | solution.py:9
  78.6 528.8 %all-reduce.2.cloned.1.call-start = ((), (), s32[]{:S(2)}) async-start(), calls=%async_computation.4 | async-start | bytes 29360128 | tf_op jit(solution)/shard_map/psum | solution.py:23
Sparse Core Ops, SparseCore 0:
  9.5 55.0 all-gather.2
  66.1 21.2 all-gather.4
  90.3 20.3 reduce-scatter.1
  113.6 493.7 all-reduce.1
where the time goes:
time: 627 us
  waiting for transfers between devices  573 us (91%)
  matrix products  27.4 us (4%)
  between operations  13.8 us (2%)
  local copies, waits for them, and re-layouts  13.2 us (2%)
    psum x1, waiting for transfers between devices, shards(): grad_weight = lax.psum(partial_sum.astype(jnp.bfloat16), 'depth')  497 us
    all_gather x1, waiting for transfers between devices, shards(): grad_rows = lax.all_gather(grad_out, 'row', axis=0, tiled=True)  55.9 us
    dot_general x1, matrix products, shards(): lax.dot_general(grad_rows, weight, (((1,), (1,)), ((), ())), preferred_el...  14 us
    dot_general x1, matrix products, shards(): lax.dot_general(lax.all_gather(acts, 'col', axis=0, tiled=True), grad_row...  13.4 us
    unnamed x1, local copies, waits for them, and re-layouts  13.2 us
  transfers between devices with their start and end apart: 4, of which 4 were waited for; matrix products, arithmetic and copies ran while one was open for 4% of the time, Pallas kernels for 0%

commit v1 on v0

v1 whole, which is shorter than its diff:
```python
import functools

import jax
import jax.numpy as jnp
from jax import lax
from jax.experimental import pallas as pl
from jax.experimental.pallas import tpu as pltpu
from jax.sharding import PartitionSpec as P

MESH = pl.DeviceIdType.MESH
CORES = 2


def kernel(nd, nr, nc, nch, cols, at_ref, g_ref, w_ref, ga_ref, gw_ref,
           grads, acts, total, term, parts, wbuf, obuf,
           recv_g, recv_a, recv_t, send_g, send_a, send_t, load_sem, w_sem, o_sem):
    nx = nr // CORES
    l, r, c = lax.axis_index("depth"), lax.axis_index("row"), lax.axis_index("col")
    core = lax.rem(r, CORES)
    xi = lax.div(r, CORES)
    partner = xi * CORES + (1 - core)
    xpeers = [lax.rem(xi + o, nx) * CORES + core for o in range(1, nx)]
    cpeers = [lax.rem(c + o, nc) for o in range(1, nc)]
    rows = g_ref.shape[0]
    width = at_ref.shape[1]
    feats = at_ref.shape[0]
    layer = nr * rows
    block = layer // nc
    UP, DOWN, CORE, X = 0, 1, 2, 3

    def piece(p, j):
        return grads.at[j, pl.ds(pl.multiple_of(p * rows, rows), rows), :]

    def whole(p):
        return grads.at[:, pl.ds(pl.multiple_of(p * rows, rows), rows), :]

    def apiece(q):
        return acts.at[:, pl.ds(pl.multiple_of(q * width, width), width)]

    def g_copy(p, j, way, dev):
        return pltpu.make_async_remote_copy(
            src_ref=piece(p, j), dst_ref=piece(p, j), send_sem=send_g.at[way, p],
            recv_sem=recv_g.at[p, j], device_id=dev, device_id_type=MESH)

    def a_copy(q, way, dev):
        return pltpu.make_async_remote_copy(
            src_ref=apiece(q), dst_ref=apiece(q), send_sem=send_a.at[way, q],
            recv_sem=recv_a.at[q], device_id=dev, device_id_type=MESH)

    def g_wait(p, j):
        pltpu.make_async_copy(piece(p, j), piece(p, j), recv_g.at[p, j]).wait()

    def a_wait(q):
        pltpu.make_async_copy(apiece(q), apiece(q), recv_a.at[q]).wait()

    def to_x(p, j):
        for o, dev in enumerate(xpeers):
            g_copy(p, j, X + o, {"row": dev}).start()

    def to_core(p, j):
        g_copy(p, j, CORE, {"row": partner}).start()

    def to_up(p, j):
        @pl.when(l < nd - 1)
        def _():
            g_copy(p, j, UP, {"depth": l + 1}).start()

    def to_down(p, j):
        @pl.when(l > 0)
        def _():
            g_copy(p, j, DOWN, {"depth": l - 1}).start()

    def w_copy(j):
        return pltpu.make_async_copy(
            w_ref.at[:, pl.ds(pl.multiple_of(j * cols, cols), cols)], wbuf.at[lax.rem(j, 2)],
            w_sem.at[lax.rem(j, 2)])

    def o_copy(j):
        return pltpu.make_async_copy(
            obuf.at[lax.rem(j, 2)], gw_ref.at[:, pl.ds(pl.multiple_of(j * cols, cols), cols)],
            o_sem.at[lax.rem(j, 2)])

    own = l * nr + r
    mine = l * nc + c

    @pl.loop(0, nch)
    def _(j):
        pltpu.make_async_copy(
            g_ref.at[:, pl.ds(pl.multiple_of(j * cols, cols), cols)], piece(own, j), load_sem.at[0]).start()

    own_acts = pltpu.make_async_copy(at_ref, apiece(mine), load_sem.at[1])
    own_acts.start()
    w_copy(0).start()

    barrier = pltpu.get_barrier_semaphore()
    peers = [{"row": partner}] + [{"row": x} for x in xpeers] + [{"col": y} for y in cpeers]
    for dev in peers:
        pl.semaphore_signal(barrier, inc=1, device_id=dev, device_id_type=MESH)

    @pl.when(l > 0)
    def _():
        pl.semaphore_signal(barrier, inc=1, device_id={"depth": l - 1}, device_id_type=MESH)

    @pl.when(l < nd - 1)
    def _():
        pl.semaphore_signal(barrier, inc=1, device_id={"depth": l + 1}, device_id_type=MESH)

    neighbours = jnp.where(l > 0, 1, 0) + jnp.where(l < nd - 1, 1, 0)
    pl.semaphore_wait(barrier, len(peers) + neighbours)

    own_acts.wait()
    pltpu.make_async_copy(whole(own), whole(own), load_sem.at[0]).wait()

    @pl.when(l < nd - 1)
    def _():
        a_copy(mine, UP, {"depth": l + 1}).start()

    @pl.when(l > 0)
    def _():
        a_copy(mine, DOWN, {"depth": l - 1}).start()

    for o, dev in enumerate(cpeers):
        a_copy(mine, 2 + o, {"col": dev}).start()

    to_up(own, 0)
    to_down(own, 0)

    @pl.loop(0, nch)
    def _(j):
        to_x(own, j)
        to_core(own, j)

    total[...] = jnp.zeros_like(total)

    tile_f = 256

    def step(s, carry):
        @pl.when(s + 1 < nch)
        def _():
            to_up(own, s + 1)
            to_down(own, s + 1)

        for d in range(1, nd):
            j = s - d
            live = (j >= 0) & (j < nch)
            for sign, onward in ((-1, to_up), (1, to_down)):
                src = l + sign * d
                there = (src >= 0) if sign < 0 else (src < nd)

                @pl.when(live & there)
                def _(j=j, src=src, onward=onward):
                    p = src * nr + r
                    g_wait(p, j)
                    onward(p, j)
                    to_x(p, j)
                    to_core(p, j)

                @pl.when((s == d) & there)
                def _(src=src, sign=sign):
                    q = src * nc + c
                    a_wait(q)
                    if sign < 0:
                        @pl.when(l < nd - 1)
                        def _():
                            a_copy(q, UP, {"depth": l + 1}).start()
                    else:
                        @pl.when(l > 0)
                        def _():
                            a_copy(q, DOWN, {"depth": l - 1}).start()
                    for o, dev in enumerate(cpeers):
                        a_copy(q, 2 + o, {"col": dev}).start()

        for d in range(0, nd):
            j = s - (d + 1 if d else 0)
            live = (j >= 0) & (j < nch)
            for sign in ((-1, 1) if d else (1,)):
                src = l + sign * d
                there = (src >= 0) & (src < nd)

                @pl.when(live & there)
                def _(j=j, src=src):
                    for x in xpeers:
                        g_wait(src * nr + x, j)
                        to_core(src * nr + x, j)

        j1 = s - 1

        @pl.when((j1 >= 0) & (j1 < nch))
        def _():
            for x in range(nx):
                g_wait(l * nr + x * CORES + 1 - core, j1)
            w_copy(j1).wait()

            @pl.when(j1 + 1 < nch)
            def _():
                w_copy(j1 + 1).start()

            lhs = grads[j1, pl.ds(pl.multiple_of(l * layer, layer), layer), :]

            @pl.loop(0, feats // tile_f)
            def _(i):
                at = pl.ds(pl.multiple_of(i * tile_f, tile_f), tile_f)
                total[:, at] += lax.dot_general(
                    lhs, wbuf[lax.rem(j1, 2), at, :], (((1,), (1,)), ((), ())),
                    preferred_element_type=jnp.float32)

        @pl.when(s == nch)
        def _():
            term[...] = total[...].astype(term.dtype)

        @pl.when(s == nch + 1)
        def _():
            for o, dev in enumerate(cpeers):
                pltpu.make_async_remote_copy(
                    src_ref=term.at[pl.ds(pl.multiple_of(dev * block, block), block), :],
                    dst_ref=parts.at[o], send_sem=send_t.at[o], recv_sem=recv_t.at[o],
                    device_id={"col": dev}, device_id_type=MESH).start()

        j2 = s - (nd + 1)

        @pl.when(j2 == 0)
        def _():
            for k in range(nd):
                for dev in cpeers:
                    a_wait(k * nc + dev)

        @pl.when(j2 >= 0)
        def _():
            for k in range(1, nd):
                for x in range(nx):
                    g_wait(lax.rem(l + k, nd) * nr + x * CORES + 1 - core, j2)

            @pl.when(j2 >= 2)
            def _():
                o_copy(j2 - 2).wait()

            @pl.loop(0, feats // tile_f)
            def _(i):
                at = pl.ds(pl.multiple_of(i * tile_f, tile_f), tile_f)
                obuf[lax.rem(j2, 2), at, :] = jnp.dot(
                    acts[at, :], grads[j2], preferred_element_type=jnp.float32).astype(obuf.dtype)

            o_copy(j2).start()

        return carry

    lax.fori_loop(0, nch + nd + 1, step, 0)

    result = total[pl.ds(pl.multiple_of(c * block, block), block), :]
    for o, dev in enumerate(cpeers):
        pltpu.make_async_copy(parts.at[o], parts.at[o], recv_t.at[o]).wait()
        result = result + parts[o].astype(jnp.float32)
    ga_ref[...] = result.astype(ga_ref.dtype)

    for o, dev in enumerate(cpeers):
        pltpu.make_async_copy(parts.at[o], parts.at[o], send_t.at[o]).wait()

    def sent_g(way, p):
        pltpu.make_async_copy(whole(p), whole(p), send_g.at[way, p]).wait()

    def sent_a(way, q):
        pltpu.make_async_copy(apiece(q), apiece(q), send_a.at[way, q]).wait()

    for k in range(nd):
        p, q = k * nr + r, k * nc + c

        @pl.when((k <= l) & (l < nd - 1))
        def _(p=p, q=q):
            sent_g(UP, p)
            sent_a(UP, q)

        @pl.when((k >= l) & (l > 0))
        def _(p=p, q=q):
            sent_g(DOWN, p)
            sent_a(DOWN, q)

        for o in range(len(xpeers)):
            sent_g(X + o, p)
        for x in range(nx):
            sent_g(CORE, k * nr + x * CORES + core)
        for o in range(len(cpeers)):
            sent_a(2 + o, q)

    if nch >= 2:
        o_copy(nch - 2).wait()
    o_copy(nch - 1).wait()


def shards(nd, nr, nc, acts, grad_out, weight):
    rows, width = grad_out.shape
    cols = 512 if width % 512 == 0 else 256
    nch = width // cols
    feats = acts.shape[1]
    layer = nr * rows
    block = layer // nc
    bf16, dma = jnp.bfloat16, pltpu.SemaphoreType.DMA
    anywhere = pl.BlockSpec(memory_space=pl.ANY)
    nx = nr // CORES
    pieces, apieces = nd * nr, nd * nc
    return pl.pallas_call(
        functools.partial(kernel, nd, nr, nc, nch, cols),
        out_shape=(
            jax.ShapeDtypeStruct((block, feats), bf16),
            jax.ShapeDtypeStruct((feats, width), bf16),
        ),
        in_specs=[anywhere] * 3,
        out_specs=(pl.BlockSpec(memory_space=pltpu.VMEM), anywhere),
        scratch_shapes=[
            pltpu.VMEM((nch, pieces * rows, cols), bf16),
            pltpu.VMEM((feats, apieces * acts.shape[0]), bf16),
            pltpu.VMEM((layer, feats), jnp.float32),
            pltpu.VMEM((layer, feats), bf16),
            pltpu.VMEM((nc - 1, block, feats), bf16),
            pltpu.VMEM((2, feats, cols), bf16),
            pltpu.VMEM((2, feats, cols), bf16),
            dma((pieces, nch)), dma((apieces,)), dma((nc - 1,)),
            dma((3 + nx - 1, pieces)), dma((2 + nc - 1, apieces)), dma((nc - 1,)),
            dma((2,)), dma((2,)), dma((2,)),
        ],
        compiler_params=pltpu.CompilerParams(
            collective_id=0, has_side_effects=True, vmem_limit_bytes=67_043_328),
    )(acts.T, grad_out, weight)


def solution(mesh):
    nd, nr, nc = mesh.shape["depth"], mesh.shape["row"], mesh.shape["col"]
    in_specs = (P(("depth", "col"), "row"), P(("depth", "row"), "col"), P("row", "col"))
    out_specs = (P(("depth", "col"), "row"), P("row", "col"))
    return jax.shard_map(functools.partial(shards, nd, nr, nc), mesh=mesh,
                         in_specs=in_specs, out_specs=out_specs, check_vma=False)
```

time: 627 us -> 197 us (0.31)
  waiting for transfers between devices: 573 us -> 0 us
  Pallas kernels: 0 us -> 179 us
  matrix products: 27.4 us -> 0 us
  between operations: 13.8 us -> 0.64 us
    psum x1 -> x0, waiting for transfers between devices: 497 us -> none  [shards(): grad_weight = lax.psum(partial_sum.astype(jnp.bfloat16), 'depth')]
    pallas_call x0 -> x1, Pallas kernels: none -> 179 us  [shards(): pl.pallas_call(functools.partial(kernel, nd, nr, nc, nch, cols), out_shap...]
    all_gather x2 -> x0, waiting for transfers between devices: 64.7 us -> none  [the longest x1 55.9 us: shards(): grad_rows = lax.all_gather(grad_out, 'row', axis=0, tiled=True)]
    dot_general x2 -> x0, matrix products: 27.4 us -> none  [the longest x1 14 us: shards(): lax.dot_general(grad_rows, weight, (((1,), (1,)), ((), ())), preferred_el...]
    reduce_scatter x1 -> x0, waiting for transfers between devices: 9.78 us -> none  [shards(): lax.psum_scatter(lax.dot_general(grad_rows, weight, (((1,), (1,)), ((), (...]
    unnamed x1 -> x3, local copies, waits for them, and re-layouts: 13.2 us -> 17.1 us
  transfers between devices with their start and end apart: 4 -> 0, of which waited for: 4 -> 0; matrix products, arithmetic and copies ran while one was open for 4% -> 0% of each run, Pallas kernels for 0% -> 0%
where the time goes in v1:
time: 197 us; the launch traced here: 196 us
  Pallas kernels  179 us (91%)
  local copies, waits for them, and re-layouts  17.1 us (9%)
    pallas_call x1, Pallas kernels, shards(): pl.pallas_call(functools.partial(kernel, nd, nr, nc, nch, cols), out_shap...  179 us
    unnamed x3, local copies, waits for them, and re-layouts  17.1 us

profile of v1, /device:TPU:0, one launch (start us, length us, event | category | flops | bytes accessed | tf_op | source)
XLA Modules:
  0.0 196.4 jit_solution(2105472305668645410)
XLA Ops:
  0.6 2.0 %copy.5 = bf16[256,1024]{0,1:T(8,128)(2,1)} copy(bf16[256,1024]{1,0:T(8,128)(2,1)} %param.3) | data formatting | bytes 1048576 | tf_op args[0]
  2.7 178.6 %shard_map.50 = (bf16[256,1024]{1,0:T(8,128)(2,1)}, bf16[1024,7168]{1,0:T(8,128)(2,1)}) custom-call(bf16[1024,256]{1,0:T(8,128)(2,1)} %bitcast.1, bf16[128,7168]{1,0:T(8,128)(2,1)} %g_ref.1, bf16[1024,7168]{1,0:T(8,128)(2,1)} %w_ref.1), custom_call_target="tpu_custom_call" | custom-call | tf_op jit(solution)/shard_map/pallas_call | solution.py:300
  181.3 1.9 copy.8
  183.1 13.2 %copy.9 = bf16[1024,7168]{1,0:T(8,128)(2,1)} copy(bf16[1024,7168]{1,0:T(8,128)(2,1)} %get-tuple-element.5) | data formatting | bytes 29360128

commit v2 on v1

--- a/solution.py
+++ b/solution.py
@@ -11,9 +11,9 @@
 CORES = 2
 
 
-def kernel(nd, nr, nc, nch, cols, at_ref, g_ref, w_ref, ga_ref, gw_ref,
+def kernel(nd, nr, nc, nch, late, cols, at_ref, g_ref, w_ref, ga_ref, gw_ref, all_ref, last_ref,
            grads, acts, total, term, parts, wbuf, obuf,
-           recv_g, recv_a, recv_t, send_g, send_a, send_t, load_sem, w_sem, o_sem):
+           recv_g, recv_a, recv_t, send_g, send_a, send_t, load_sem, w_sem, o_sem, all_sem, last_sem):
     nx = nr // CORES
     l, r, c = lax.axis_index("depth"), lax.axis_index("row"), lax.axis_index("col")
     core = lax.rem(r, CORES)
@@ -79,6 +79,13 @@
         return pltpu.make_async_copy(
             obuf.at[lax.rem(j, 2)], gw_ref.at[:, pl.ds(pl.multiple_of(j * cols, cols), cols)],
             o_sem.at[lax.rem(j, 2)])
+
+    def last_copy(i):
+        return pltpu.make_async_copy(
+            grads.at[nch - late + i], last_ref.at[:, pl.ds(pl.multiple_of(i * cols, cols), cols)],
+            last_sem.at[i])
+
+    all_copy = pltpu.make_async_copy(acts, all_ref, all_sem)
 
     own = l * nr + r
     mine = l * nc + c
@@ -223,6 +230,7 @@
             for k in range(nd):
                 for dev in cpeers:
                     a_wait(k * nc + dev)
+            all_copy.start()
 
         @pl.when(j2 >= 0)
         def _():
@@ -230,6 +238,12 @@
                 for x in range(nx):
                     g_wait(lax.rem(l + k, nd) * nr + x * CORES + 1 - core, j2)
 
+            @pl.when(j2 >= nch - late)
+            def _():
+                last_copy(j2 - (nch - late)).start()
+
+        @pl.when((j2 >= 0) & (j2 < nch - late))
+        def _():
             @pl.when(j2 >= 2)
             def _():
                 o_copy(j2 - 2).wait()
@@ -281,15 +295,76 @@
         for o in range(len(cpeers)):
             sent_a(2 + o, q)
 
-    if nch >= 2:
-        o_copy(nch - 2).wait()
-    o_copy(nch - 1).wait()
+    for j in range(max(nch - late - 2, 0), nch - late):
+        o_copy(j).wait()
+    all_copy.wait()
+    for i in range(late):
+        last_copy(i).wait()
+
+
+def finish(tile, ga_ref, done_ref, all_ref, last_ref, ga_out, gw_out,
+           gbuf, dbuf, abuf, lbuf, tail, g_sem, in_sem, a_sem, l_sem, out_sem, t_sem):
+    feats, early = done_ref.shape
+    tiles = feats // tile
+    width = gw_out.shape[1]
+
+    def rows(i):
+        return pl.ds(pl.multiple_of(i * tile, tile), tile)
+
+    def a_in(i):
+        return pltpu.make_async_copy(all_ref.at[rows(i), :], abuf.at[rows(i), :], a_sem.at[i])
+
+    def d_in(i):
+        return pltpu.make_async_copy(done_ref.at[rows(i), :], dbuf.at[rows(i), :], in_sem.at[i])
+
+    def d_out(i):
+        return pltpu.make_async_copy(
+            dbuf.at[rows(i), :], gw_out.at[rows(i), pl.ds(0, early)], out_sem.at[i])
+
+    def t_out(i):
+        return pltpu.make_async_copy(
+            tail.at[rows(i), :], gw_out.at[rows(i), pl.ds(early, width - early)], t_sem.at[i])
+
+    l_in = pltpu.make_async_copy(last_ref, lbuf, l_sem)
+    g_in = pltpu.make_async_copy(ga_ref, gbuf, g_sem.at[0])
+    g_out = pltpu.make_async_copy(gbuf, ga_out, g_sem.at[1])
+    d_in(0).start()
+    l_in.start()
+    a_in(0).start()
+    g_in.start()
+    for i in range(1, tiles):
+        a_in(i).start()
+        d_in(i).start()
+    d_in(0).wait()
+    d_out(0).start()
+    l_in.wait()
+    g_in.wait()
+    g_out.start()
+
+    @pl.loop(0, tiles)
+    def _(i):
+        @pl.when(i > 0)
+        def _():
+            d_in(i).wait()
+            d_out(i).start()
+
+        a_in(i).wait()
+        tail[rows(i), :] = jnp.dot(
+            abuf[rows(i), :], lbuf[...], preferred_element_type=jnp.float32).astype(tail.dtype)
+        t_out(i).start()
+
+    g_out.wait()
+    for i in range(tiles):
+        d_out(i).wait()
+        t_out(i).wait()
 
 
 def shards(nd, nr, nc, acts, grad_out, weight):
     rows, width = grad_out.shape
-    cols = 512 if width % 512 == 0 else 256
+    cols = 256
     nch = width // cols
+    late = min(4, nch - 2)
+    early = (nch - late) * cols
     feats = acts.shape[1]
     layer = nr * rows
     block = layer // nc
@@ -297,14 +372,18 @@
     anywhere = pl.BlockSpec(memory_space=pl.ANY)
     nx = nr // CORES
     pieces, apieces = nd * nr, nd * nc
-    return pl.pallas_call(
-        functools.partial(kernel, nd, nr, nc, nch, cols),
+    tokens = nd * layer
+    limit = 67_043_328
+    ga, done, all_acts, last = pl.pallas_call(
+        functools.partial(kernel, nd, nr, nc, nch, late, cols),
         out_shape=(
             jax.ShapeDtypeStruct((block, feats), bf16),
-            jax.ShapeDtypeStruct((feats, width), bf16),
+            jax.ShapeDtypeStruct((feats, early), bf16),
+            jax.ShapeDtypeStruct((feats, tokens), bf16),
+            jax.ShapeDtypeStruct((tokens, late * cols), bf16),
         ),
         in_specs=[anywhere] * 3,
-        out_specs=(pl.BlockSpec(memory_space=pltpu.VMEM), anywhere),
+        out_specs=(pl.BlockSpec(memory_space=pltpu.VMEM),) + (anywhere,) * 3,
         scratch_shapes=[
             pltpu.VMEM((nch, pieces * rows, cols), bf16),
             pltpu.VMEM((feats, apieces * acts.shape[0]), bf16),
@@ -315,11 +394,31 @@
             pltpu.VMEM((2, feats, cols), bf16),
             dma((pieces, nch)), dma((apieces,)), dma((nc - 1,)),
             dma((3 + nx - 1, pieces)), dma((2 + nc - 1, apieces)), dma((nc - 1,)),
-            dma((2,)), dma((2,)), dma((2,)),
+            dma((2,)), dma((2,)), dma((2,)), dma, dma((late,)),
         ],
         compiler_params=pltpu.CompilerParams(
-            collective_id=0, has_side_effects=True, vmem_limit_bytes=67_043_328),
+            collective_id=0, has_side_effects=True, vmem_limit_bytes=limit),
     )(acts.T, grad_out, weight)
+    tile = 256
+    tiles = feats // tile
+    return pl.pallas_call(
+        functools.partial(finish, tile),
+        out_shape=(
+            jax.ShapeDtypeStruct((block, feats), bf16),
+            jax.ShapeDtypeStruct((feats, width), bf16),
+        ),
+        in_specs=[anywhere] * 4,
+        out_specs=(anywhere,) * 2,
+        scratch_shapes=[
+            pltpu.VMEM((block, feats), bf16),
+            pltpu.VMEM((feats, early), bf16),
+            pltpu.VMEM((feats, tokens), bf16),
+            pltpu.VMEM((tokens, width - early), bf16),
+            pltpu.VMEM((feats, width - early), bf16),
+            dma((2,)), dma((tiles,)), dma((tiles,)), dma, dma((tiles,)), dma((tiles,)),
+        ],
+        compiler_params=pltpu.CompilerParams(vmem_limit_bytes=limit),
+    )(ga, done, all_acts, last)
 
 
 def solution(mesh):

time: 197 us -> 202 us (1.025)
  Pallas kernels: 179 us -> 200 us
  local copies, waits for them, and re-layouts: 17.1 us -> 2.04 us
    pallas_call x1 -> x2, Pallas kernels: 179 us -> 200 us  [the longest x1 187 us: shards(): pl.pallas_call(functools.partial(kernel, nd, nr, nc, nch, late, cols), ou...]
    unnamed x3 -> x1, local copies, waits for them, and re-layouts: 17.1 us -> 2.04 us
where the time goes in v2:
time: 202 us
  Pallas kernels  200 us (99%)
  local copies, waits for them, and re-layouts  2.04 us (1%)
    pallas_call x1, Pallas kernels, shards(): pl.pallas_call(functools.partial(kernel, nd, nr, nc, nch, late, cols), ou...  187 us
    pallas_call x1, Pallas kernels, shards(): pl.pallas_call(functools.partial(finish, tile), out_shape=(jax.ShapeDtype...  13 us

profile of v2, /device:TPU:0, one launch (start us, length us, event | category | flops | bytes accessed | tf_op | source)
XLA Modules:
  0.0 202.2 jit_solution(15271009329192789368)
XLA Ops:
  0.6 2.0 %copy.5 = bf16[256,1024]{0,1:T(8,128)(2,1)} copy(bf16[256,1024]{1,0:T(8,128)(2,1)} %param.3) | data formatting | bytes 1048576 | tf_op args[0]
  2.7 186.5 %shard_map.50 = (bf16[256,1024]{1,0:T(8,128)(2,1)}, bf16[1024,6144]{1,0:T(8,128)(2,1)}, bf16[1024,2048]{1,0:T(8,128)(2,1)}, bf16[2048,1024]{1,0:T(8,128)(2,1)}) custom-call(bf16[1024,256]{1,0:T(8,128)(2,1)} %bitcast.1, bf16[128,7168]{1,0:T(8,128)(2,1)} %g_ref.1, bf16[1024,7168]{1,0:T(8,128)(2,1)} %w_ref.1), custom_call_target="tpu_custom_call" | custom-call | tf_op jit(solution)/shard_map/pallas_call | solution.py:377
  189.2 13.0 %shard_map.51 = (bf16[256,1024]{1,0:T(8,128)(2,1)}, bf16[1024,7168]{1,0:T(8,128)(2,1)}) custom-call(bf16[256,1024]{1,0:T(8,128)(2,1)} %get-tuple-element.6.ga_ref, bf16[1024,6144]{1,0:T(8,128)(2,1)} %get-tuple-element.7.done_ref, bf16[1024,2048]{1,0:T(8,128)(2,1)} %get-tuple-element.8.all_ref, bf16[2048,1024]{1,0:T(8,128)(2,1)} %get-tuple-element.9.last_ref), custom_call_target="tpu_custom_call" | custom-call | tf_op jit(solution)/shard_map/pallas_call | solution.py:404

commit v3 on v2

--- a/solution.py
+++ b/solution.py
@@ -129,8 +129,9 @@
     for o, dev in enumerate(cpeers):
         a_copy(mine, 2 + o, {"col": dev}).start()
 
-    to_up(own, 0)
-    to_down(own, 0)
+    for j in range(min(1, nch)):
+        to_up(own, j)
+        to_down(own, j)
 
     @pl.loop(0, nch)
     def _(j):
@@ -361,9 +362,9 @@
 
 def shards(nd, nr, nc, acts, grad_out, weight):
     rows, width = grad_out.shape
-    cols = 256
+    cols = 512 if width % 512 == 0 else 256
     nch = width // cols
-    late = min(4, nch - 2)
+    late = max(min(2, nch - 2), 1)
     early = (nch - late) * cols
     feats = acts.shape[1]
     layer = nr * rows

time: 202 us -> 191 us (0.946); the launches traced: 202 us -> 189 us
  Pallas kernels: 200 us -> 186 us
    pallas_call x1, Pallas kernels: 187 us -> 173 us  [shards(): pl.pallas_call(functools.partial(kernel, nd, nr, nc, nch, late, cols), ou...]
where the time goes in v3:
time: 191 us; the launch traced here: 189 us
  Pallas kernels  186 us (97%)
  local copies, waits for them, and re-layouts  2.04 us (1%)
    pallas_call x1, Pallas kernels, shards(): pl.pallas_call(functools.partial(kernel, nd, nr, nc, nch, late, cols), ou...  173 us
    pallas_call x1, Pallas kernels, shards(): pl.pallas_call(functools.partial(finish, tile), out_shape=(jax.ShapeDtype...  13 us

profile of v3, /device:TPU:0, one launch (start us, length us, event | category | flops | bytes accessed | tf_op | source)
XLA Modules:
  0.0 189.2 jit_solution(2787195639033193430)
XLA Ops:
  0.6 2.0 %copy.5 = bf16[256,1024]{0,1:T(8,128)(2,1)} copy(bf16[256,1024]{1,0:T(8,128)(2,1)} %param.3) | data formatting | bytes 1048576 | tf_op args[0]
  2.7 173.5 %shard_map.50 = (bf16[256,1024]{1,0:T(8,128)(2,1)}, bf16[1024,6144]{1,0:T(8,128)(2,1)}, bf16[1024,2048]{1,0:T(8,128)(2,1)}, bf16[2048,1024]{1,0:T(8,128)(2,1)}) custom-call(bf16[1024,256]{1,0:T(8,128)(2,1)} %bitcast.1, bf16[128,7168]{1,0:T(8,128)(2,1)} %g_ref.1, bf16[1024,7168]{1,0:T(8,128)(2,1)} %w_ref.1), custom_call_target="tpu_custom_call" | custom-call | tf_op jit(solution)/shard_map/pallas_call | solution.py:378
  176.2 13.0 %shard_map.51 = (bf16[256,1024]{1,0:T(8,128)(2,1)}, bf16[1024,7168]{1,0:T(8,128)(2,1)}) custom-call(bf16[256,1024]{1,0:T(8,128)(2,1)} %get-tuple-element.6.ga_ref, bf16[1024,6144]{1,0:T(8,128)(2,1)} %get-tuple-element.7.done_ref, bf16[1024,2048]{1,0:T(8,128)(2,1)} %get-tuple-element.8.all_ref, bf16[2048,1024]{1,0:T(8,128)(2,1)} %get-tuple-element.9.last_ref), custom_call_target="tpu_custom_call" | custom-call | tf_op jit(solution)/shard_map/pallas_call | solution.py:405
